TPU v7x, 32 devices: a whole 2x2x4 slice. The times are simulated.
32 devices in a mesh: gy: 16 (over z, y, core), gz: 2 (over x).
Axes of the slice: x: 2, y: 2, z: 4, core: 2. Of those that a mesh axis runs over, the one named last changes fastest.
Arguments:
- initial_block: bfloat16 [16, 2, 2, 512, 512], P('gy', 'gz'), may hold values from -6 to 6
- tile_ops: bfloat16 [16, 2, 2, 512, 512], P('gy', 'gz'), may hold values from -0.125 to 0.125
- couple_ops: bfloat16 [16, 2, 4, 2, 512, 512], P('gy', 'gz'), may hold values from -0.125 to 0.125
- couple_map: int32 [16, 2, 4, 2], P('gy', 'gz'), may hold values from 0 to 1
- cell_scale: float32 [16, 2, 2, 512], P('gy', 'gz'), may hold values from 0.4 to 2.5
Outputs:
- basis: float32 [16, 2, 2, 512, 512], P('gy', 'gz')
- factor: float32 [512, 512], replicated
All inputs are finite; a program needn't handle non-finite values.
Results may differ from a plain program's by a relative error of at most 0.0053.
Values may be sent and summed in bfloat16 or wider, within the bound.
A program may use at most 64 MiB of HBM per device.

v0:
```python
import jax
import jax.numpy as jnp
from jax import lax
from jax.sharding import PartitionSpec as P


def shifted(block, axis, distance):
    devices = range(lax.axis_size(axis))
    route = [((i - distance) % len(devices), i) for i in devices]
    return lax.ppermute(block, axis, route)


def pick_tiles(blocks, indices):
    return jnp.take(blocks, indices, axis=0)


def neighbour_faces(scaled):
    y_from_lower = shifted(scaled, "gy", 1)
    y_from_upper = shifted(scaled, "gy", -1)
    z_from_lower = shifted(scaled, "gz", 1)
    z_from_upper = shifted(scaled, "gz", -1)
    faces = [y_from_lower[0, 0], y_from_upper[0, 0], z_from_lower[0, 0], z_from_upper[0, 0]]
    return jnp.stack(faces)


def apply_scaled(field, tile_ops, couple_ops, couple_map, cell_scale):
    scale_wide = cell_scale[..., None]
    scaled = (scale_wide * field).astype(jnp.bfloat16)
    inner = jnp.einsum(
        "tij,tjk->tik", tile_ops[0, 0], scaled[0, 0], preferred_element_type=jnp.float32
    )
    stacked = neighbour_faces(scaled)
    picked = jax.vmap(pick_tiles)(stacked, couple_map[0, 0])
    outer = jnp.einsum(
        "dtij,dtjk->tik", couple_ops[0, 0], picked, preferred_element_type=jnp.float32
    )
    return scale_wide * (inner + outer)[None, None]


def body(initial_block, tile_ops, couple_ops, couple_map, cell_scale):

    def filter_map(field):
        return (
            (1.0 - 1.1) * field - apply_scaled(field, tile_ops, couple_ops, couple_map, cell_scale)
        ) / 0.9

    first = initial_block.astype(jnp.float32)
    second = filter_map(first)
    third = 2.0 * filter_map(second) - first
    fourth = 2.0 * filter_map(third) - second
    width = fourth.shape[-1]
    flat = fourth.reshape(-1, width)
    total_cells = flat.shape[0] * lax.axis_size("gy") * lax.axis_size("gz")
    local_gram = jnp.einsum("ck,cl->kl", flat, flat, precision=lax.Precision.HIGHEST)
    gram = lax.psum(local_gram, ("gy", "gz"))
    gram = gram / jnp.float32(total_cells)
    lower = jnp.linalg.cholesky(gram)
    basis = jax.scipy.linalg.solve_triangular(lower, flat.T, lower=True).T
    return (basis.reshape(fourth.shape), lower.T)


def solution(mesh):
    placed = (
        P("gy", "gz", None, None, None),
        P("gy", "gz", None, None, None),
        P("gy", "gz", None, None, None, None),
        P("gy", "gz", None, None),
        P("gy", "gz", None, None),
    )
    return jax.shard_map(
        body,
        mesh=mesh,
        in_specs=placed,
        out_specs=(P("gy", "gz", None, None, None), P()),
        check_vma=False,
    )
```

profile of v0, /device:TPU:0, one launch (start us, length us, event | category | flops | bytes accessed | tf_op | source)
XLA Modules:
  0.0 432.5 jit_solution(8653095912852456125)
XLA Ops:
  7.2 1.6 fusion.10
  8.8 0.5 collective-permute-start
  9.4 5.0 %collective-permute-start.1 = (bf16[1,1,2,512,512]{4,3,2,1,0:T(8,128)(2,1)S(1)}, bf16[1,1,2,512,512]{4,3,2,1,0:T(8,128)(2,1)}, u32[]{:S(2)}, u32[]{:S(2)}) collective-permute-start(bf16[1,1,2,512,512]{4,3,2,1,0:T(8,128)(2,1)S(1)} %fusion.10), channel_id=1, source_target_pairs={{2,0},{4,2},{6,4},{8,6},{10,8},{12,10},{14,12},{16,14},{18,16},{20... | collective-permute-start | bytes 3145736 | tf_op jit(solution)/shard_map/ppermute | solution.py:10
  14.4 1.9 collective-permute-start.2
  16.5 2.0 fusion.48
  18.6 8.4 %collective-permute-done = bf16[1,1,2,512,512]{4,3,2,1,0:T(8,128)(2,1)S(1)} collective-permute-done((bf16[1,1,2,512,512]{4,3,2,1,0:T(8,128)(2,1)S(1)}, bf16[1,1,2,512,512]{4,3,2,1,0:T(8,128)(2,1)S(1)}, u32[]{:S(2)}, u32[]{:S(2)}) %collective-permute-start) | collective-permute-done | bytes 1048608 | tf_op jit(solution)/shard_map/ppermute | solution.py:10
  27.0 10.2 %collective-permute-done.2 = bf16[1,1,2,512,512]{4,3,2,1,0:T(8,128)(2,1)} collective-permute-done((bf16[1,1,2,512,512]{4,3,2,1,0:T(8,128)(2,1)S(1)}, bf16[1,1,2,512,512]{4,3,2,1,0:T(8,128)(2,1)}, u32[]{:S(2)}, u32[]{:S(2)}) %collective-permute-start.2) | collective-permute-done | bytes 1048608 | tf_op jit(solution)/shard_map/ppermute | solution.py:10
  37.2 3.9 pad_maximum_fusion
  41.1 5.1 %gather_fusion = bf16[8,512,512]{2,1,0:T(8,128)(2,1)} fusion(bf16[4,2,512,512]{3,2,1,0:T(8,128)(2,1)} %pad_maximum_fusion, s32[8]{0:T(128)S(1)} %reshape.120), kind=kCustom, calls=%fused_computation.clone | custom fusion | bytes 8388672 | tf_op jit(solution)/shard_map/vmap(jit(_take))/gather | solution.py:14
  46.2 7.5 %multiply_convert_fusion.1 = (bf16[1,1,2,512,512]{4,3,2,1,0:T(8,128)(2,1)S(1)}, f32[1,1,2,512,512]{4,3,2,1,0:T(8,128)}) fusion(f32[2,512]{1,0:T(2,128)S(1)} %broadcast_multiply_fusion.1, f32[2,512,512]{1,2,0:T(8,128)S(1)} %copy-done.4, bf16[4,2,512,512]{3,2,1,0:T(8,128)(2,1)} %bitcast.157, pred[4,2]{0,1:T(4,128)(4,1)S(1)} %compare_and_fusion, ...), kind=kOutput, calls=%fused_computation.43 | convolution fusion | flops 2153250816 | bytes 14688264 | tf_op jit(solution)/shard_map/dtij,dtjk->tik/dot_general | solution.py:34
  53.8 0.4 collective-permute-start.3
  54.2 4.0 collective-permute-start.4
  58.2 1.5 collective-permute-start.5
  59.7 0.7 fusion.46
  60.4 10.4 %collective-permute-done.3 = bf16[1,1,2,512,512]{4,3,2,1,0:T(8,128)(2,1)S(1)} collective-permute-done((bf16[1,1,2,512,512]{4,3,2,1,0:T(8,128)(2,1)S(1)}, bf16[1,1,2,512,512]{4,3,2,1,0:T(8,128)(2,1)S(1)}, u32[]{:S(2)}, u32[]{:S(2)}) %collective-permute-start.3) | collective-permute-done | bytes 1048608 | tf_op jit(solution)/shard_map/ppermute | solution.py:10
  70.8 9.7 %collective-permute-done.5 = bf16[1,1,2,512,512]{4,3,2,1,0:T(8,128)(2,1)S(1)} collective-permute-done((bf16[1,1,2,512,512]{4,3,2,1,0:T(8,128)(2,1)S(1)}, bf16[1,1,2,512,512]{4,3,2,1,0:T(8,128)(2,1)S(1)}, u32[]{:S(2)}, u32[]{:S(2)}) %collective-permute-start.5) | collective-permute-done | bytes 1048608 | tf_op jit(solution)/shard_map/ppermute | solution.py:10
  80.5 2.3 pad_maximum_fusion.1
  82.7 4.9 %gather_fusion.1 = bf16[8,512,512]{2,1,0:T(8,128)(2,1)} fusion(bf16[4,2,512,512]{3,2,1,0:T(8,128)(2,1)} %pad_maximum_fusion.1, s32[8]{0:T(128)S(1)} %reshape.120), kind=kCustom, calls=%fused_computation.1.clone | custom fusion | bytes 8388672 | tf_op jit(solution)/shard_map/vmap(jit(_take))/gather | solution.py:14
  87.7 8.4 %multiply_convert_fusion = (bf16[1,1,2,512,512]{4,3,2,1,0:T(8,128)(2,1)S(1)}, f32[1,1,2,512,512]{4,3,2,1,0:T(8,128)}) fusion(f32[2,512]{1,0:T(2,128)S(1)} %bitcast.173, bf16[1,1,2,512,512]{4,3,2,1,0:T(8,128)(2,1)} %param.7, f32[2,512,512]{1,2,0:T(8,128)S(1)} %fusion.46, bf16[4,2,512,512]{3,2,1,0:T(8,128)(2,1)} %bitcast.158, ...), kind=kOutput, calls=%fused_computation.42 | convolution fusion | flops 2154299392 | bytes 16781320 | tf_op jit(solution)/shard_map/dtij,dtjk->tik/dot_general | solution.py:34
  96.1 0.4 collective-permute-start.6
  96.5 4.0 collective-permute-start.7
  100.6 1.5 collective-permute-start.8
  102.0 0.7 fusion.44
  102.8 10.4 %collective-permute-done.6 = bf16[1,1,2,512,512]{4,3,2,1,0:T(8,128)(2,1)S(1)} collective-permute-done((bf16[1,1,2,512,512]{4,3,2,1,0:T(8,128)(2,1)S(1)}, bf16[1,1,2,512,512]{4,3,2,1,0:T(8,128)(2,1)S(1)}, u32[]{:S(2)}, u32[]{:S(2)}) %collective-permute-start.6) | collective-permute-done | bytes 1048608 | tf_op jit(solution)/shard_map/ppermute | solution.py:10
  113.1 9.7 %collective-permute-done.8 = bf16[1,1,2,512,512]{4,3,2,1,0:T(8,128)(2,1)S(1)} collective-permute-done((bf16[1,1,2,512,512]{4,3,2,1,0:T(8,128)(2,1)S(1)}, bf16[1,1,2,512,512]{4,3,2,1,0:T(8,128)(2,1)S(1)}, u32[]{:S(2)}, u32[]{:S(2)}) %collective-permute-start.8) | collective-permute-done | bytes 1048608 | tf_op jit(solution)/shard_map/ppermute | solution.py:10
  122.8 2.4 pad_maximum_fusion.2
  125.2 4.9 %gather_fusion.2 = bf16[8,512,512]{2,1,0:T(8,128)(2,1)} fusion(bf16[4,2,512,512]{3,2,1,0:T(8,128)(2,1)} %pad_maximum_fusion.2, s32[8]{0:T(128)S(1)} %reshape.120), kind=kCustom, calls=%fused_computation.2.clone | custom fusion | bytes 8388672 | tf_op jit(solution)/shard_map/vmap(jit(_take))/gather | solution.py:14
  130.2 7.3 %fusion.12 = f32[1,1,2,512,512]{4,3,2,1,0:T(8,128)S(1)} fusion(f32[2,512,512]{1,2,0:T(8,128)S(1)} %fusion.44, f32[1,1,2,512,512]{4,3,2,1,0:T(8,128)} %get-tuple-element.38, f32[1,1,2,512,512]{4,3,2,1,0:T(8,128)} %get-tuple-element.40, bf16[4,2,512,512]{3,2,1,0:T(8,128)(2,1)} %bitcast.156, pred[4,2]{0,1:T(4,128)(4,1)S(1)} %compare_and_fusion, ...), kind=kOutput, calls=%fused_computation.28 | convolution fusion | flops 2153250816 | bytes 16781320 | tf_op jit(solution)/shard_map/dtij,dtjk->tik/dot_general | solution.py:34
  137.5 1.3 copy-done.3
  138.8 4.5 %fusion.28 = f32[512,512]{0,1:T(8,128)} fusion(f32[1,1,2,512,512]{4,3,2,1,0:T(8,128)S(1)} %fusion.12), kind=kOutput, calls=%fused_computation.50 | convolution fusion | flops 3221225472 | bytes 3145728 | tf_op jit(solution)/shard_map/ck,cl->kl/dot_general | solution.py:54
  143.4 130.6 %all-reduce.3.cloned.1.call-done = f32[512,512]{0,1:T(8,128)} async-done(((f32[512,512]{0,1:T(8,128)}), f32[512,512]{0,1:T(8,128)}) %all-reduce.3.cloned.1.call-update) | async-done | bytes 1048592 | tf_op jit(solution)/shard_map/psum | solution.py:55
  274.0 1.4 broadcast_multiply_fusion
  276.0 11.7 %cholesky.104 = f32[128,128]{1,0:T(8,128)S(1)} custom-call(f32[128,128]{1,0:T(8,128)S(1)} %cholesky.266), custom_call_target="Cholesky" | custom-call | tf_op jit(solution)/shard_map/jit(cholesky)/cholesky | solution.py:57
  287.9 10.0 %custom-call.31 = f32[1,128,128]{1,2,0:T(8,128)S(1)} custom-call(f32[1,128,128]{2,1,0:T(8,128)S(1)} %get-tuple-element.36), custom_call_target="InvertDiagBlocksLowerTriangular" | custom-call | tf_op jit(solution)/shard_map/jit(cholesky)/cholesky | solution.py:57
  298.6 11.7 %cholesky.217 = f32[128,128]{1,0:T(8,128)S(1)} custom-call(f32[128,128]{1,0:T(8,128)S(1)} %cholesky.270), custom_call_target="Cholesky" | custom-call | tf_op jit(solution)/shard_map/jit(cholesky)/cholesky | solution.py:57
  310.3 9.8 %custom-call.32 = f32[1,128,128]{1,2,0:T(8,128)S(1)} custom-call(f32[1,128,128]{2,1,0:T(8,128)S(1)} %get-tuple-element.33), custom_call_target="InvertDiagBlocksLowerTriangular" | custom-call | tf_op jit(solution)/shard_map/jit(cholesky)/cholesky | solution.py:57
  320.4 0.4 convolution_subtract_fusion.3
  320.8 11.7 %cholesky.238 = f32[128,128]{1,0:T(8,128)S(1)} custom-call(f32[128,128]{1,0:T(8,128)S(1)} %cholesky.275), custom_call_target="Cholesky" | custom-call | tf_op jit(solution)/shard_map/jit(cholesky)/cholesky | solution.py:57
  332.6 0.7 compare_reduce_fusion.1
  333.3 10.2 %custom-call.33 = f32[1,128,128]{1,2,0:T(8,128)S(1)} custom-call(f32[1,128,128]{2,1,0:T(8,128)S(1)} %get-tuple-element.30), custom_call_target="InvertDiagBlocksLowerTriangular" | custom-call | tf_op jit(solution)/shard_map/jit(cholesky)/cholesky | solution.py:57
  343.7 0.4 convolution_subtract_fusion.4
  344.0 11.7 %cholesky.255 = f32[128,128]{1,0:T(8,128)S(1)} custom-call(f32[128,128]{1,0:T(8,128)S(1)} %convolution_subtract_fusion.4), custom_call_target="Cholesky" | custom-call | tf_op jit(solution)/shard_map/jit(cholesky)/cholesky | solution.py:57
  355.8 0.7 compare_reduce_fusion
  356.4 0.6 compare_reduce_fusion.2
  359.5 1.2 fusion.54
  360.8 8.4 %while.1 = (s32[]{:T(128)}, f32[512,512]{1,0:T(8,128)S(1)}, s32[4,2]{0,1:T(2,128)S(1)}, f32[4,128,128]{2,1,0:T(8,128)S(1)}, s32[]{:T(128)}) while((s32[]{:T(128)}, f32[512,512]{1,0:T(8,128)S(1)}, s32[4,2]{0,1:T(2,128)S(1)}, f32[4,128,128]{2,1,0:T(8,128)S(1)}, s32[]{:T(128)}) %tuple.37), condition=%wide.while_cond, body=%wide.while_body.sunk | while | flops 2 | bytes 131181 | solution.py:58
  360.8 0.6 fusion.89
  361.4 1.4 bitcast_dynamic-update-slice_fusion.2
  362.9 0.6 fusion.89
  363.5 1.4 bitcast_dynamic-update-slice_fusion.2
  365.0 0.6 fusion.89
  365.6 1.4 bitcast_dynamic-update-slice_fusion.2
  367.1 0.6 fusion.89
  367.7 1.4 bitcast_dynamic-update-slice_fusion.2
  369.2 39.5 %custom-call.34 = f32[4,128,128]{1,2,0:T(8,128)S(1)} custom-call(f32[4,128,128]{2,1,0:T(8,128)S(1)} %get-tuple-element.10), custom_call_target="InvertDiagBlocksLowerTriangular" | custom-call | tf_op jit(solution)/shard_map/jit(_solve_triangular)/triangular_solve | solution.py:58
  408.6 1.7 fusion.55
  410.3 2.0 convolution_subtract_fusion.1
  412.4 0.6 fusion.68
  413.0 2.9 convolution_subtract_fusion
  415.9 0.6 fusion.66
  416.5 3.8 fusion.37
  420.3 0.6 fusion.65
  421.1 1.8 copy.41
  422.9 2.5 copy.34
  (45 shorter events, 2.7 us)
Async XLA Ops:
  7.2 9.4 %copy-start = (bf16[1,1,2,512,512]{4,3,2,1,0:T(8,128)(2,1)S(1)}, bf16[1,1,2,512,512]{4,3,2,1,0:T(8,128)(2,1)}, u32[]{:S(2)}) copy-start(bf16[1,1,2,512,512]{4,3,2,1,0:T(8,128)(2,1)} %param.8) | copy-start | bytes 3145732
  7.2 9.3 %copy-start.5 = (f32[1,1,2,512]{3,2,1,0:T(2,128)S(1)}, f32[1,1,2,512]{3,2,1,0:T(2,128)}, u32[]{:S(2)}) copy-start(f32[1,1,2,512]{3,2,1,0:T(2,128)} %param.11) | copy-start | bytes 12292
  7.2 9.1 %copy-start.6 = (s32[1,1,4,2]{2,3,1,0:T(2,128)S(1)}, s32[1,1,4,2]{2,3,1,0:T(2,128)}, u32[]{:S(2)}) copy-start(s32[1,1,4,2]{2,3,1,0:T(2,128)} %param.10) | copy-start | bytes 100
  7.2 266.8 %all-reduce.3.cloned.1.call-start = ((), (), s32[]{:S(2)}) async-start(), calls=%async_computation | async-start | bytes 2097152 | tf_op jit(solution)/shard_map/psum | solution.py:55
  8.8 18.1 %collective-permute-start = (bf16[1,1,2,512,512]{4,3,2,1,0:T(8,128)(2,1)S(1)}, bf16[1,1,2,512,512]{4,3,2,1,0:T(8,128)(2,1)S(1)}, u32[]{:S(2)}, u32[]{:S(2)}) collective-permute-start(bf16[1,1,2,512,512]{4,3,2,1,0:T(8,128)(2,1)S(1)} %fusion.10), channel_id=1, source_target_pairs={{30,0},{0,2},{2,4},{4,6},{6,8},{8,10},{10,12},{12,14},{14,16},{16,... | collective-permute-start | bytes 3145736 | tf_op jit(solution)/shard_map/ppermute | solution.py:10
  9.4 17.6 %collective-permute-start.1 = (bf16[1,1,2,512,512]{4,3,2,1,0:T(8,128)(2,1)S(1)}, bf16[1,1,2,512,512]{4,3,2,1,0:T(8,128)(2,1)}, u32[]{:S(2)}, u32[]{:S(2)}) collective-permute-start(bf16[1,1,2,512,512]{4,3,2,1,0:T(8,128)(2,1)S(1)} %fusion.10), channel_id=1, source_target_pairs={{2,0},{4,2},{6,4},{8,6},{10,8},{12,10},{14,12},{16,14},{18,16},{20... | collective-permute-start | bytes 3145736 | tf_op jit(solution)/shard_map/ppermute | solution.py:10
  14.4 22.7 %collective-permute-start.2 = (bf16[1,1,2,512,512]{4,3,2,1,0:T(8,128)(2,1)S(1)}, bf16[1,1,2,512,512]{4,3,2,1,0:T(8,128)(2,1)}, u32[]{:S(2)}, u32[]{:S(2)}) collective-permute-start(bf16[1,1,2,512,512]{4,3,2,1,0:T(8,128)(2,1)S(1)} %fusion.10), channel_id=1, source_target_pairs={{1,0},{0,1},{3,2},{2,3},{5,4},{4,5},{7,6},{6,7},{9,8},{8,9},{11,10... | collective-permute-start | bytes 3145736 | tf_op jit(solution)/shard_map/ppermute | solution.py:10
  41.1 5.1 %copy-start.4 = (f32[2,512,512]{1,2,0:T(8,128)S(1)}, f32[2,512,512]{1,2,0:T(8,128)}, u32[]{:S(2)}) copy-start(f32[2,512,512]{1,2,0:T(8,128)} %fusion.48) | copy-start | bytes 6291460
  53.8 17.0 %collective-permute-start.3 = (bf16[1,1,2,512,512]{4,3,2,1,0:T(8,128)(2,1)S(1)}, bf16[1,1,2,512,512]{4,3,2,1,0:T(8,128)(2,1)S(1)}, u32[]{:S(2)}, u32[]{:S(2)}) collective-permute-start(bf16[1,1,2,512,512]{4,3,2,1,0:T(8,128)(2,1)S(1)} %get-tuple-element.37), channel_id=1, source_target_pairs={{30,0},{0,2},{2,4},{4,6},{6,8},{8,10},{10,12},{12,14},{14,16},{16,... | collective-permute-start | bytes 3145736 | tf_op jit(solution)/shard_map/ppermute | solution.py:10
  54.2 16.6 %collective-permute-start.4 = (bf16[1,1,2,512,512]{4,3,2,1,0:T(8,128)(2,1)S(1)}, bf16[1,1,2,512,512]{4,3,2,1,0:T(8,128)(2,1)S(1)}, u32[]{:S(2)}, u32[]{:S(2)}) collective-permute-start(bf16[1,1,2,512,512]{4,3,2,1,0:T(8,128)(2,1)S(1)} %get-tuple-element.37), channel_id=1, source_target_pairs={{2,0},{4,2},{6,4},{8,6},{10,8},{12,10},{14,12},{16,14},{18,16},{20... | collective-permute-start | bytes 3145736 | tf_op jit(solution)/shard_map/ppermute | solution.py:10
  58.2 22.3 %collective-permute-start.5 = (bf16[1,1,2,512,512]{4,3,2,1,0:T(8,128)(2,1)S(1)}, bf16[1,1,2,512,512]{4,3,2,1,0:T(8,128)(2,1)S(1)}, u32[]{:S(2)}, u32[]{:S(2)}) collective-permute-start(bf16[1,1,2,512,512]{4,3,2,1,0:T(8,128)(2,1)S(1)} %get-tuple-element.37), channel_id=1, source_target_pairs={{1,0},{0,1},{3,2},{2,3},{5,4},{4,5},{7,6},{6,7},{9,8},{8,9},{11,10... | collective-permute-start | bytes 3145736 | tf_op jit(solution)/shard_map/ppermute | solution.py:10
  96.1 17.0 %collective-permute-start.6 = (bf16[1,1,2,512,512]{4,3,2,1,0:T(8,128)(2,1)S(1)}, bf16[1,1,2,512,512]{4,3,2,1,0:T(8,128)(2,1)S(1)}, u32[]{:S(2)}, u32[]{:S(2)}) collective-permute-start(bf16[1,1,2,512,512]{4,3,2,1,0:T(8,128)(2,1)S(1)} %get-tuple-element.39), channel_id=1, source_target_pairs={{30,0},{0,2},{2,4},{4,6},{6,8},{8,10},{10,12},{12,14},{14,16},{16,... | collective-permute-start | bytes 3145736 | tf_op jit(solution)/shard_map/ppermute | solution.py:10
  96.5 16.6 %collective-permute-start.7 = (bf16[1,1,2,512,512]{4,3,2,1,0:T(8,128)(2,1)S(1)}, bf16[1,1,2,512,512]{4,3,2,1,0:T(8,128)(2,1)S(1)}, u32[]{:S(2)}, u32[]{:S(2)}) collective-permute-start(bf16[1,1,2,512,512]{4,3,2,1,0:T(8,128)(2,1)S(1)} %get-tuple-element.39), channel_id=1, source_target_pairs={{2,0},{4,2},{6,4},{8,6},{10,8},{12,10},{14,12},{16,14},{18,16},{20... | collective-permute-start | bytes 3145736 | tf_op jit(solution)/shard_map/ppermute | solution.py:10
  100.6 22.3 %collective-permute-start.8 = (bf16[1,1,2,512,512]{4,3,2,1,0:T(8,128)(2,1)S(1)}, bf16[1,1,2,512,512]{4,3,2,1,0:T(8,128)(2,1)S(1)}, u32[]{:S(2)}, u32[]{:S(2)}) collective-permute-start(bf16[1,1,2,512,512]{4,3,2,1,0:T(8,128)(2,1)S(1)} %get-tuple-element.39), channel_id=1, source_target_pairs={{1,0},{0,1},{3,2},{2,3},{5,4},{4,5},{7,6},{6,7},{9,8},{8,9},{11,10... | collective-permute-start | bytes 3145736 | tf_op jit(solution)/shard_map/ppermute | solution.py:10
  137.5 1.3 copy-start.3
  274.0 1.8 copy-start.2
  421.1 4.4 %copy-start.1 = (bf16[1,1,2,512,512]{4,3,2,1,0:T(8,128)(2,1)S(1)}, bf16[1,1,2,512,512]{4,3,2,1,0:T(8,128)(2,1)}, u32[]{:S(2)}) copy-start(bf16[1,1,2,512,512]{4,3,2,1,0:T(8,128)(2,1)} %param.8) | copy-start | bytes 3145732
Sparse Core Ops, SparseCore 0:
  143.5 130.4 all-reduce.2
where the time goes:
time: 439 us; the launch traced here: 432 us
  waiting for transfers between devices  189 us (43%)
  other arithmetic  132 us (30%)
  matrix products  45.4 us (10%)
  local copies, waits for them, and re-layouts  29.7 us (7%)
  starting transfers between devices  19.4 us (4%)
  between operations  17 us (4%)
    psum x1, waiting for transfers between devices, body(): gram = lax.psum(local_gram, ('gy', 'gz'))  131 us
    another operation x14, other arithmetic, body(): lower = jnp.linalg.cholesky(gram)  78.9 us
    ppermute x9, waiting for transfers between devices, shifted(): return lax.ppermute(block, axis, route)  58.7 us
    another operation x2, other arithmetic, body(): basis = jax.scipy.linalg.solve_triangular(lower, flat.T, lower=True).T  39.5 us
    dot_general x3, matrix products, apply_scaled(): jnp.einsum('dtij,dtjk->tik', couple_ops[0, 0], picked, preferred_element_...  23.3 us
    ppermute x9, starting transfers between devices, shifted(): return lax.ppermute(block, axis, route)  19.3 us
    gather x5, local copies, waits for them, and re-layouts, pick_tiles(): return jnp.take(blocks, indices, axis=0)  15.2 us
    another operation x7, matrix products, body(): basis = jax.scipy.linalg.solve_triangular(lower, flat.T, lower=True).T  12.3 us
  transfers between devices with their start and end apart: 10, of which 7 were waited for; matrix products, arithmetic and copies ran while one was open for 1% of the time, Pallas kernels for 0%

commit v1 on v0

--- a/solution.py
+++ b/solution.py
@@ -52,7 +52,7 @@
     flat = fourth.reshape(-1, width)
     total_cells = flat.shape[0] * lax.axis_size("gy") * lax.axis_size("gz")
     local_gram = jnp.einsum("ck,cl->kl", flat, flat, precision=lax.Precision.HIGHEST)
-    gram = lax.psum(local_gram, ("gy", "gz"))
+    gram = jnp.sum(lax.all_gather(local_gram, ("gy", "gz")), axis=0)
     gram = gram / jnp.float32(total_cells)
     lower = jnp.linalg.cholesky(gram)
     basis = jax.scipy.linalg.solve_triangular(lower, flat.T, lower=True).T

time: 439 us -> 523 us (1.19)
  waiting for transfers between devices: 189 us -> 251 us
  other arithmetic: 132 us -> 145 us
  local copies, waits for them, and re-layouts: 29.7 us -> 38.9 us
    all_gather x0 -> x1, waiting for transfers between devices: none -> 192 us  [body(): gram = jnp.sum(lax.all_gather(local_gram, ('gy', 'gz')), axis=0)]
    psum x1 -> x0, waiting for transfers between devices: 131 us -> none  [body(): gram = lax.psum(local_gram, ('gy', 'gz'))]
    reduce_sum x0 -> x1, other arithmetic: none -> 12.4 us  [body(): gram = jnp.sum(lax.all_gather(local_gram, ('gy', 'gz')), axis=0)]
    another operation x12, local copies, waits for them, and re-layouts: 8.31 us -> 13.7 us
  transfers between devices with their start and end apart: 10 -> 10, of which waited for: 7 -> 8; matrix products, arithmetic and copies ran while one was open for 1% -> 1% of each run, Pallas kernels for 0% -> 0%
where the time goes in v1:
time: 523 us; the launch traced here: 516 us
  waiting for transfers between devices  251 us (48%)
  other arithmetic  145 us (28%)
  matrix products  44.3 us (8%)
  local copies, waits for them, and re-layouts  38.9 us (7%)
  starting transfers between devices  19.9 us (4%)
  between operations  17.3 us (3%)
    all_gather x1, waiting for transfers between devices, body(): gram = jnp.sum(lax.all_gather(local_gram, ('gy', 'gz')), axis=0)  192 us
    another operation x14, other arithmetic, body(): lower = jnp.linalg.cholesky(gram)  78.6 us
    ppermute x9, waiting for transfers between devices, shifted(): return lax.ppermute(block, axis, route)  58.8 us
    another operation x2, other arithmetic, body(): basis = jax.scipy.linalg.solve_triangular(lower, flat.T, lower=True).T  40.1 us
    dot_general x3, matrix products, apply_scaled(): jnp.einsum('dtij,dtjk->tik', couple_ops[0, 0], picked, preferred_element_...  23.3 us
    ppermute x9, starting transfers between devices, shifted(): return lax.ppermute(block, axis, route)  19.8 us
    gather x5, local copies, waits for them, and re-layouts, pick_tiles(): return jnp.take(blocks, indices, axis=0)  15.2 us
    another operation x12, local copies, waits for them, and re-layouts  13.7 us
  transfers between devices with their start and end apart: 10, of which 8 were waited for; matrix products, arithmetic and copies ran while one was open for 1% of the time, Pallas kernels for 0%

profile of v1, /device:TPU:0, one launch (start us, length us, event | category | flops | bytes accessed | tf_op | source)
XLA Modules:
  0.0 516.0 jit_solution(2633133458906682429)
XLA Ops:
  7.2 1.6 fusion.10
  8.8 0.5 collective-permute-start
  9.4 5.0 collective-permute-start.1
  14.4 1.9 collective-permute-start.2
  16.5 2.0 fusion.48
  18.6 8.4 %collective-permute-done = bf16[1,1,2,512,512]{4,3,2,1,0:T(8,128)(2,1)S(1)} collective-permute-done((bf16[1,1,2,512,512]{4,3,2,1,0:T(8,128)(2,1)S(1)}, bf16[1,1,2,512,512]{4,3,2,1,0:T(8,128)(2,1)S(1)}, u32[]{:S(2)}, u32[]{:S(2)}) %collective-permute-start) | collective-permute-done | bytes 1048608 | tf_op jit(solution)/shard_map/ppermute | solution.py:10
  27.0 10.2 %collective-permute-done.2 = bf16[1,1,2,512,512]{4,3,2,1,0:T(8,128)(2,1)} collective-permute-done((bf16[1,1,2,512,512]{4,3,2,1,0:T(8,128)(2,1)S(1)}, bf16[1,1,2,512,512]{4,3,2,1,0:T(8,128)(2,1)}, u32[]{:S(2)}, u32[]{:S(2)}) %collective-permute-start.2) | collective-permute-done | bytes 1048608 | tf_op jit(solution)/shard_map/ppermute | solution.py:10
  37.2 3.9 pad_maximum_fusion
  41.1 5.1 gather_fusion
  46.2 7.5 %multiply_convert_fusion.1 = (bf16[1,1,2,512,512]{4,3,2,1,0:T(8,128)(2,1)S(1)}, f32[1,1,2,512,512]{4,3,2,1,0:T(8,128)}) fusion(f32[2,512]{1,0:T(2,128)S(1)} %broadcast_multiply_fusion, f32[2,512,512]{1,2,0:T(8,128)S(1)} %copy-done.3, bf16[4,2,512,512]{3,2,1,0:T(8,128)(2,1)} %bitcast.162, pred[4,2]{0,1:T(4,128)(4,1)S(1)} %compare_and_fusion, ...), kind=kOutput, calls=%fused_computation.43 | convolution fusion | flops 2153250816 | bytes 14688264 | tf_op jit(solution)/shard_map/dtij,dtjk->tik/dot_general | solution.py:34
  54.2 4.0 collective-permute-start.4
  58.2 1.5 collective-permute-start.5
  59.7 0.7 fusion.46
  60.4 10.4 %collective-permute-done.3 = bf16[1,1,2,512,512]{4,3,2,1,0:T(8,128)(2,1)S(1)} collective-permute-done((bf16[1,1,2,512,512]{4,3,2,1,0:T(8,128)(2,1)S(1)}, bf16[1,1,2,512,512]{4,3,2,1,0:T(8,128)(2,1)S(1)}, u32[]{:S(2)}, u32[]{:S(2)}) %collective-permute-start.3) | collective-permute-done | bytes 1048608 | tf_op jit(solution)/shard_map/ppermute | solution.py:10
  70.8 9.7 %collective-permute-done.5 = bf16[1,1,2,512,512]{4,3,2,1,0:T(8,128)(2,1)S(1)} collective-permute-done((bf16[1,1,2,512,512]{4,3,2,1,0:T(8,128)(2,1)S(1)}, bf16[1,1,2,512,512]{4,3,2,1,0:T(8,128)(2,1)S(1)}, u32[]{:S(2)}, u32[]{:S(2)}) %collective-permute-start.5) | collective-permute-done | bytes 1048608 | tf_op jit(solution)/shard_map/ppermute | solution.py:10
  80.5 2.3 pad_maximum_fusion.1
  82.7 4.9 gather_fusion.1
  87.7 8.4 %multiply_convert_fusion = (bf16[1,1,2,512,512]{4,3,2,1,0:T(8,128)(2,1)S(1)}, f32[1,1,2,512,512]{4,3,2,1,0:T(8,128)}) fusion(f32[2,512]{1,0:T(2,128)S(1)} %bitcast.175, bf16[1,1,2,512,512]{4,3,2,1,0:T(8,128)(2,1)} %param.7, f32[2,512,512]{1,2,0:T(8,128)S(1)} %fusion.46, bf16[4,2,512,512]{3,2,1,0:T(8,128)(2,1)} %bitcast.163, ...), kind=kOutput, calls=%fused_computation.42 | convolution fusion | flops 2154299392 | bytes 16781320 | tf_op jit(solution)/shard_map/dtij,dtjk->tik/dot_general | solution.py:34
  96.5 4.5 collective-permute-start.7
  101.1 1.5 collective-permute-start.8
  102.5 0.7 fusion.44
  103.3 9.9 %collective-permute-done.6 = bf16[1,1,2,512,512]{4,3,2,1,0:T(8,128)(2,1)S(1)} collective-permute-done((bf16[1,1,2,512,512]{4,3,2,1,0:T(8,128)(2,1)S(1)}, bf16[1,1,2,512,512]{4,3,2,1,0:T(8,128)(2,1)S(1)}, u32[]{:S(2)}, u32[]{:S(2)}) %collective-permute-start.6) | collective-permute-done | bytes 1048608 | tf_op jit(solution)/shard_map/ppermute | solution.py:10
  113.4 10.0 %collective-permute-done.8 = bf16[1,1,2,512,512]{4,3,2,1,0:T(8,128)(2,1)S(1)} collective-permute-done((bf16[1,1,2,512,512]{4,3,2,1,0:T(8,128)(2,1)S(1)}, bf16[1,1,2,512,512]{4,3,2,1,0:T(8,128)(2,1)S(1)}, u32[]{:S(2)}, u32[]{:S(2)}) %collective-permute-start.8) | collective-permute-done | bytes 1048608 | tf_op jit(solution)/shard_map/ppermute | solution.py:10
  123.4 2.3 pad_maximum_fusion.2
  125.7 4.9 gather_fusion.2
  130.6 7.3 %fusion.12 = f32[1,1,2,512,512]{4,3,2,1,0:T(8,128)S(1)} fusion(f32[2,512,512]{1,2,0:T(8,128)S(1)} %fusion.44, f32[1,1,2,512,512]{4,3,2,1,0:T(8,128)} %get-tuple-element.40, f32[1,1,2,512,512]{4,3,2,1,0:T(8,128)} %get-tuple-element.42, bf16[4,2,512,512]{3,2,1,0:T(8,128)(2,1)} %bitcast.161, pred[4,2]{0,1:T(4,128)(4,1)S(1)} %compare_and_fusion, ...), kind=kOutput, calls=%fused_computation.28 | convolution fusion | flops 2153250816 | bytes 16781320 | tf_op jit(solution)/shard_map/dtij,dtjk->tik/dot_general | solution.py:34
  137.9 1.3 copy-done.4
  139.2 4.5 fusion.28
  143.8 1.9 copy.44
  145.7 192.3 %all-gather.3.cloned.1.call-done = f32[16384,512]{1,0:T(8,128)} async-done(((f32[512,512]{1,0:T(8,128)}), f32[16384,512]{1,0:T(8,128)}) %all-gather.3.cloned.1.call-update) | async-done | bytes 33554448 | tf_op jit(solution)/shard_map/all_gather | solution.py:55
  338.0 12.4 %reduce_sum.11 = f32[512,512]{1,0:T(8,128)S(1)} reduce(f32[32,512,512]{2,1,0:T(8,128)} %bitcast.156, f32[]{:T(128)} %constant.165.clone.1), dimensions={0}, to_apply=%region_0.0 | reduce | flops 8126464 | bytes 34603012 | tf_op jit(solution)/shard_map/reduce_sum | solution.py:55
  350.4 1.3 copy.43
  351.8 1.4 fusion.43
  353.2 1.0 copy-done.2
  354.2 11.7 %cholesky.104 = f32[128,128]{1,0:T(8,128)S(1)} custom-call(f32[128,128]{1,0:T(8,128)S(1)} %cholesky.266), custom_call_target="Cholesky" | custom-call | tf_op jit(solution)/shard_map/jit(cholesky)/cholesky | solution.py:57
  366.1 9.8 %custom-call.31 = f32[1,128,128]{1,2,0:T(8,128)S(1)} custom-call(f32[1,128,128]{2,1,0:T(8,128)S(1)} %get-tuple-element.38), custom_call_target="InvertDiagBlocksLowerTriangular" | custom-call | tf_op jit(solution)/shard_map/jit(cholesky)/cholesky | solution.py:57
  375.9 1.2 constant_dynamic-update-slice_fusion.3
  377.1 1.3 convolution_subtract_fusion.2
  378.4 11.7 %cholesky.217 = f32[128,128]{1,0:T(8,128)S(1)} custom-call(f32[128,128]{1,0:T(8,128)S(1)} %cholesky.270), custom_call_target="Cholesky" | custom-call | tf_op jit(solution)/shard_map/jit(cholesky)/cholesky | solution.py:57
  390.2 10.0 %custom-call.32 = f32[1,128,128]{1,2,0:T(8,128)S(1)} custom-call(f32[1,128,128]{2,1,0:T(8,128)S(1)} %get-tuple-element.35), custom_call_target="InvertDiagBlocksLowerTriangular" | custom-call | tf_op jit(solution)/shard_map/jit(cholesky)/cholesky | solution.py:57
  400.4 1.3 convolution_subtract_fusion.3
  401.7 11.7 %cholesky.238 = f32[128,128]{1,0:T(8,128)S(1)} custom-call(f32[128,128]{1,0:T(8,128)S(1)} %cholesky.275), custom_call_target="Cholesky" | custom-call | tf_op jit(solution)/shard_map/jit(cholesky)/cholesky | solution.py:57
  413.5 0.7 compare_reduce_fusion.1
  414.2 9.8 %custom-call.33 = f32[1,128,128]{1,2,0:T(8,128)S(1)} custom-call(f32[1,128,128]{2,1,0:T(8,128)S(1)} %get-tuple-element.32), custom_call_target="InvertDiagBlocksLowerTriangular" | custom-call | tf_op jit(solution)/shard_map/jit(cholesky)/cholesky | solution.py:57
  424.2 1.2 convolution_subtract_fusion.4
  425.4 11.7 %cholesky.255 = f32[128,128]{1,0:T(8,128)S(1)} custom-call(f32[128,128]{1,0:T(8,128)S(1)} %convolution_subtract_fusion.4), custom_call_target="Cholesky" | custom-call | tf_op jit(solution)/shard_map/jit(cholesky)/cholesky | solution.py:57
  437.2 0.7 compare_reduce_fusion
  437.8 0.6 compare_reduce_fusion.2
  441.0 1.8 fusion.54
  442.8 13.7 %while.1 = (s32[]{:T(128)}, f32[512,512]{1,0:T(8,128)}, s32[4,2]{0,1:T(2,128)S(1)}, f32[4,128,128]{2,1,0:T(8,128)}, s32[]{:T(128)}) while((s32[]{:T(128)}, f32[512,512]{1,0:T(8,128)}, s32[4,2]{0,1:T(2,128)S(1)}, f32[4,128,128]{2,1,0:T(8,128)}, s32[]{:T(128)}) %tuple.38), condition=%wide.while_cond, body=%wide.while_body.sunk | while | flops 2 | bytes 132705 | solution.py:58
  443.4 2.8 bitcast_dynamic-update-slice_fusion.2
  446.8 2.8 bitcast_dynamic-update-slice_fusion.2
  450.2 2.8 bitcast_dynamic-update-slice_fusion.2
  453.7 2.8 bitcast_dynamic-update-slice_fusion.2
  456.4 40.1 %custom-call.34 = f32[4,128,128]{1,2,0:T(8,128)S(1)} custom-call(f32[4,128,128]{2,1,0:T(8,128)} %get-tuple-element.10), custom_call_target="InvertDiagBlocksLowerTriangular" | custom-call | tf_op jit(solution)/shard_map/jit(_solve_triangular)/triangular_solve | solution.py:58
  496.6 0.6 fusion.55
  497.2 1.4 convolution_subtract_fusion.1
  498.6 0.6 fusion.68
  499.3 1.6 convolution_subtract_fusion
  500.9 0.6 fusion.66
  501.5 2.0 fusion.37
  503.6 0.6 fusion.65
  504.4 1.8 copy.51
  506.2 2.5 copy.46
  (46 shorter events, 4.6 us)
Async XLA Ops:
  7.2 9.4 %copy-start = (bf16[1,1,2,512,512]{4,3,2,1,0:T(8,128)(2,1)S(1)}, bf16[1,1,2,512,512]{4,3,2,1,0:T(8,128)(2,1)}, u32[]{:S(2)}) copy-start(bf16[1,1,2,512,512]{4,3,2,1,0:T(8,128)(2,1)} %param.8) | copy-start | bytes 3145732
  7.2 9.3 %copy-start.5 = (f32[1,1,2,512]{3,2,1,0:T(2,128)S(1)}, f32[1,1,2,512]{3,2,1,0:T(2,128)}, u32[]{:S(2)}) copy-start(f32[1,1,2,512]{3,2,1,0:T(2,128)} %param.11) | copy-start | bytes 12292
  7.2 9.1 %copy-start.6 = (s32[1,1,4,2]{2,3,1,0:T(2,128)S(1)}, s32[1,1,4,2]{2,3,1,0:T(2,128)}, u32[]{:S(2)}) copy-start(s32[1,1,4,2]{2,3,1,0:T(2,128)} %param.10) | copy-start | bytes 100
  7.2 330.8 %all-gather.3.cloned.1.call-start = ((), (), s32[]{:S(2)}) async-start(), calls=%async_computation | async-start | bytes 34603008 | tf_op jit(solution)/shard_map/all_gather | solution.py:55
  8.8 18.1 %collective-permute-start = (bf16[1,1,2,512,512]{4,3,2,1,0:T(8,128)(2,1)S(1)}, bf16[1,1,2,512,512]{4,3,2,1,0:T(8,128)(2,1)S(1)}, u32[]{:S(2)}, u32[]{:S(2)}) collective-permute-start(bf16[1,1,2,512,512]{4,3,2,1,0:T(8,128)(2,1)S(1)} %fusion.10), channel_id=1, source_target_pairs={{30,0},{0,2},{2,4},{4,6},{6,8},{8,10},{10,12},{12,14},{14,16},{16,... | collective-permute-start | bytes 3145736 | tf_op jit(solution)/shard_map/ppermute | solution.py:10
  9.4 17.6 %collective-permute-start.1 = (bf16[1,1,2,512,512]{4,3,2,1,0:T(8,128)(2,1)S(1)}, bf16[1,1,2,512,512]{4,3,2,1,0:T(8,128)(2,1)}, u32[]{:S(2)}, u32[]{:S(2)}) collective-permute-start(bf16[1,1,2,512,512]{4,3,2,1,0:T(8,128)(2,1)S(1)} %fusion.10), channel_id=1, source_target_pairs={{2,0},{4,2},{6,4},{8,6},{10,8},{12,10},{14,12},{16,14},{18,16},{20... | collective-permute-start | bytes 3145736 | tf_op jit(solution)/shard_map/ppermute | solution.py:10
  14.4 22.7 %collective-permute-start.2 = (bf16[1,1,2,512,512]{4,3,2,1,0:T(8,128)(2,1)S(1)}, bf16[1,1,2,512,512]{4,3,2,1,0:T(8,128)(2,1)}, u32[]{:S(2)}, u32[]{:S(2)}) collective-permute-start(bf16[1,1,2,512,512]{4,3,2,1,0:T(8,128)(2,1)S(1)} %fusion.10), channel_id=1, source_target_pairs={{1,0},{0,1},{3,2},{2,3},{5,4},{4,5},{7,6},{6,7},{9,8},{8,9},{11,10... | collective-permute-start | bytes 3145736 | tf_op jit(solution)/shard_map/ppermute | solution.py:10
  41.1 5.1 copy-start.3
  53.8 17.0 %collective-permute-start.3 = (bf16[1,1,2,512,512]{4,3,2,1,0:T(8,128)(2,1)S(1)}, bf16[1,1,2,512,512]{4,3,2,1,0:T(8,128)(2,1)S(1)}, u32[]{:S(2)}, u32[]{:S(2)}) collective-permute-start(bf16[1,1,2,512,512]{4,3,2,1,0:T(8,128)(2,1)S(1)} %get-tuple-element.39), channel_id=1, source_target_pairs={{30,0},{0,2},{2,4},{4,6},{6,8},{8,10},{10,12},{12,14},{14,16},{16,... | collective-permute-start | bytes 3145736 | tf_op jit(solution)/shard_map/ppermute | solution.py:10
  54.2 16.6 %collective-permute-start.4 = (bf16[1,1,2,512,512]{4,3,2,1,0:T(8,128)(2,1)S(1)}, bf16[1,1,2,512,512]{4,3,2,1,0:T(8,128)(2,1)S(1)}, u32[]{:S(2)}, u32[]{:S(2)}) collective-permute-start(bf16[1,1,2,512,512]{4,3,2,1,0:T(8,128)(2,1)S(1)} %get-tuple-element.39), channel_id=1, source_target_pairs={{2,0},{4,2},{6,4},{8,6},{10,8},{12,10},{14,12},{16,14},{18,16},{20... | collective-permute-start | bytes 3145736 | tf_op jit(solution)/shard_map/ppermute | solution.py:10
  58.2 22.3 %collective-permute-start.5 = (bf16[1,1,2,512,512]{4,3,2,1,0:T(8,128)(2,1)S(1)}, bf16[1,1,2,512,512]{4,3,2,1,0:T(8,128)(2,1)S(1)}, u32[]{:S(2)}, u32[]{:S(2)}) collective-permute-start(bf16[1,1,2,512,512]{4,3,2,1,0:T(8,128)(2,1)S(1)} %get-tuple-element.39), channel_id=1, source_target_pairs={{1,0},{0,1},{3,2},{2,3},{5,4},{4,5},{7,6},{6,7},{9,8},{8,9},{11,10... | collective-permute-start | bytes 3145736 | tf_op jit(solution)/shard_map/ppermute | solution.py:10
  96.1 17.0 %collective-permute-start.6 = (bf16[1,1,2,512,512]{4,3,2,1,0:T(8,128)(2,1)S(1)}, bf16[1,1,2,512,512]{4,3,2,1,0:T(8,128)(2,1)S(1)}, u32[]{:S(2)}, u32[]{:S(2)}) collective-permute-start(bf16[1,1,2,512,512]{4,3,2,1,0:T(8,128)(2,1)S(1)} %get-tuple-element.41), channel_id=1, source_target_pairs={{30,0},{0,2},{2,4},{4,6},{6,8},{8,10},{10,12},{12,14},{14,16},{16,... | collective-permute-start | bytes 3145736 | tf_op jit(solution)/shard_map/ppermute | solution.py:10
  96.5 16.9 %collective-permute-start.7 = (bf16[1,1,2,512,512]{4,3,2,1,0:T(8,128)(2,1)S(1)}, bf16[1,1,2,512,512]{4,3,2,1,0:T(8,128)(2,1)S(1)}, u32[]{:S(2)}, u32[]{:S(2)}) collective-permute-start(bf16[1,1,2,512,512]{4,3,2,1,0:T(8,128)(2,1)S(1)} %get-tuple-element.41), channel_id=1, source_target_pairs={{2,0},{4,2},{6,4},{8,6},{10,8},{12,10},{14,12},{16,14},{18,16},{20... | collective-permute-start | bytes 3145736 | tf_op jit(solution)/shard_map/ppermute | solution.py:10
  101.1 22.3 %collective-permute-start.8 = (bf16[1,1,2,512,512]{4,3,2,1,0:T(8,128)(2,1)S(1)}, bf16[1,1,2,512,512]{4,3,2,1,0:T(8,128)(2,1)S(1)}, u32[]{:S(2)}, u32[]{:S(2)}) collective-permute-start(bf16[1,1,2,512,512]{4,3,2,1,0:T(8,128)(2,1)S(1)} %get-tuple-element.41), channel_id=1, source_target_pairs={{1,0},{0,1},{3,2},{2,3},{5,4},{4,5},{7,6},{6,7},{9,8},{8,9},{11,10... | collective-permute-start | bytes 3145736 | tf_op jit(solution)/shard_map/ppermute | solution.py:10
  137.9 1.3 copy-start.4
  353.2 1.0 copy-start.2
  504.4 4.4 copy-start.1
Sparse Core Ops, SparseCore 0:
  143.9 194.0 all-gather.2
